TPU v7x, 32 devices: a whole 2x2x4 slice. The times are simulated.
32 devices in a mesh: dp: 8 (over z, x), rep: 4 (over y, core).
Axes of the slice: x: 2, y: 2, z: 4, core: 2. Of those that a mesh axis runs over, the one named last changes fastest.
Arguments:
- hot_ids: int32 [8192, 2], P(('dp', 'rep')), may hold values from 0 to 1023
- cold_owner: int32 [16384, 1], P(('dp', 'rep')), may hold values from 0 to 7; in each aligned block of 512 rows (0 to 511, 512 to 1023, ...) at most 128 rows name the same one
- cold_offset: int32 [16384], P(('dp', 'rep')), may hold values from 0 to 511
- labels: int32 [8192], P(('dp', 'rep')), may hold values 0 or 1
- top_weight: bfloat16 [512, 1024], replicated, may hold values from -0.25 to 0.25
- out_weight: float32 [1024], replicated, may hold values from -0.5 to 0.5
- cold_table: float32 [4096, 128], P('dp'), may hold values from -6 to 6
- cold_accum: float32 [4096, 128], P('dp'), may hold values from 0.0001 to 0.01
- hot_cache: float32 [1024, 128], replicated, may hold values from -6 to 6
- hot_accum: float32 [1024, 128], replicated, may hold values from 0.01 to 1
- pending: float32 [32768, 128], P(('dp', 'rep')), may hold values from -0.3 to 0.3
- refresh_blocks: int32 [3], replicated, may hold values from 0 to 7, as said below
- block_clock: int32 [8], replicated, may hold values from 0 to 8
Outputs:
- cold_table_new: float32 [4096, 128], P('dp')
- cold_accum_new: float32 [4096, 128], P('dp')
- hot_cache_new: float32 [1024, 128], replicated
- hot_accum_new: float32 [1024, 128], replicated
- pending_new: float32 [32768, 128], P(('dp', 'rep'))
- top_grad: float32 [512, 1024], P(('dp', 'rep'))
- out_grad: float32 [1024], replicated
Inputs may be any that keep to these rules, and one draw needn't show every extreme that they name: `cold_owner`: within the lookups of one device (512 rows), no owner is named more than 128 times. `refresh_blocks`: the block numbers are distinct.
All inputs are finite; a program needn't handle non-finite values. No bound on the sum of `labels` on one device may be relied on, other than what follows from the above.
Results may differ from a plain program's by a relative error of at most 0.00165.
The roundings to bfloat16 on the way count: a program that leaves them out, or rounds other values in their place, can miss the bound.
Values may be sent and summed in bfloat16 or wider, within the bound.
A program may use at most 64 MiB of HBM per device.

v0:
```python
import jax
import jax.numpy as jnp
from jax import lax
from jax.sharding import PartitionSpec as P

BLOCK = 128
step_size = 0.5
epsilon = 1e-08


def adagrad(table_rows, accum_rows, gradient):
    accum_next = accum_rows + gradient * gradient
    return (table_rows - step_size * gradient / (jnp.sqrt(accum_next) + epsilon), accum_next)


def local(
    hot_ids,
    cold_owner,
    cold_offset,
    labels,
    top_weight,
    out_weight,
    cold_table,
    cold_accum,
    hot_cache,
    hot_accum,
    pending,
    refresh_blocks,
    block_clock,
):
    width = hot_cache.shape[1]
    samples = hot_ids.shape[0]
    hot_feats = hot_ids.shape[1]
    lookups = cold_offset.shape[0]
    cold_feats = lookups // samples
    owners_count = lax.axis_size("dp")
    capacity = max(2, 2 * lookups // owners_count)
    owners = cold_owner[:, 0]
    matches = (owners[:, None] == jnp.arange(owners_count, dtype=jnp.int32)[None, :]).astype(
        jnp.int32
    )
    earlier = jnp.cumsum(matches, axis=0) - matches
    positions = jnp.sum(earlier * matches, axis=1)
    targets = owners * capacity + positions
    requests = jnp.zeros((owners_count * capacity,), jnp.int32).at[targets].set(cold_offset)
    requests = requests.reshape(owners_count, capacity)
    asked = lax.all_to_all(requests, "dp", split_axis=0, concat_axis=0, tiled=True)
    found = cold_table[asked].astype(jnp.bfloat16)
    returned = lax.all_to_all(found, "dp", split_axis=0, concat_axis=0, tiled=True)
    cold_rows = returned.reshape(owners_count * capacity, width)[targets]
    cold_rows = cold_rows.reshape(samples, cold_feats, width)
    hot_rows = hot_cache[hot_ids].astype(jnp.bfloat16)
    inputs = jnp.concatenate([hot_rows, cold_rows], axis=1).reshape(
        samples, (hot_feats + cold_feats) * width
    )
    preact = jnp.dot(inputs, top_weight, preferred_element_type=jnp.float32)
    hidden = jax.nn.silu(preact).astype(jnp.bfloat16)
    hidden_wide = hidden.astype(jnp.float32)
    logits = jnp.dot(hidden_wide, out_weight, precision=lax.Precision.HIGHEST)
    errors = jax.nn.sigmoid(logits) - labels.astype(jnp.float32)
    gates = jax.nn.sigmoid(preact)
    slope = gates * (1.0 + preact * (1.0 - gates))
    dhidden = (errors[:, None] * out_weight[None, :] * slope).astype(jnp.bfloat16)
    head_term = jnp.dot(errors, hidden_wide, precision=lax.Precision.HIGHEST)
    top_grad = lax.psum_scatter(
        lax.dot_general(
            inputs, dhidden, (((0,), (0,)), ((), ())), preferred_element_type=jnp.float32
        ),
        ("dp", "rep"),
        scatter_dimension=0,
        tiled=True,
    )
    dinputs = lax.dot_general(
        dhidden, top_weight, (((1,), (1,)), ((), ())), preferred_element_type=jnp.float32
    ).astype(jnp.bfloat16)
    dinputs = dinputs.reshape(samples, hot_feats + cold_feats, width)
    cold_dx = dinputs[:, hot_feats:].reshape(lookups, width)
    outgoing = jnp.zeros((owners_count * capacity, width), jnp.bfloat16).at[targets].set(cold_dx)
    outgoing = outgoing.reshape(owners_count, capacity, width)
    incoming = lax.all_to_all(outgoing, "dp", split_axis=0, concat_axis=0, tiled=True)
    own_rows = cold_table.shape[0]
    cold_grad = (
        jnp.zeros((own_rows, width), jnp.float32)
        .at[asked.reshape(-1)]
        .add(incoming.reshape(-1, width).astype(jnp.float32))
    )
    quarter = own_rows // lax.axis_size("rep")
    offset_rows = lax.axis_index("rep") * quarter
    cold_share = lax.psum_scatter(cold_grad, "rep", scatter_dimension=0, tiled=True)
    table_share = lax.dynamic_slice_in_dim(cold_table, offset_rows, quarter, 0)
    accum_share = lax.dynamic_slice_in_dim(cold_accum, offset_rows, quarter, 0)
    table_updated, accum_updated = adagrad(table_share, accum_share, cold_share)
    cold_table_new, cold_accum_new = (
        lax.all_gather(table_updated, "rep", axis=0, tiled=True),
        lax.all_gather(accum_updated, "rep", axis=0, tiled=True),
    )
    hot_count = hot_cache.shape[0]
    blocks_count = hot_count // BLOCK
    hot_dx = dinputs[:, :hot_feats].reshape(samples * hot_feats, width).astype(jnp.float32)
    hot_grad = jnp.zeros((hot_count, width), jnp.float32).at[hot_ids.reshape(-1)].add(hot_dx)
    carried = (pending + hot_grad).reshape(blocks_count, BLOCK, width)
    picked = carried[refresh_blocks]
    divisors = 1.0 + block_clock[refresh_blocks].astype(jnp.float32)
    cache_blocks = hot_cache.reshape(blocks_count, BLOCK, width)
    accum_blocks = hot_accum.reshape(blocks_count, BLOCK, width)
    cache_chosen = cache_blocks[refresh_blocks]
    accum_chosen = accum_blocks[refresh_blocks]
    picked_sum, out_grad = lax.psum((picked, head_term), ("dp", "rep"))
    flush = picked_sum / divisors[:, None, None]
    cache_part, accum_part = adagrad(cache_chosen, accum_chosen, flush)
    hot_cache_new = cache_blocks.at[refresh_blocks].set(cache_part).reshape(hot_count, width)
    hot_accum_new = accum_blocks.at[refresh_blocks].set(accum_part).reshape(hot_count, width)
    pending_new = carried.at[refresh_blocks].set(0.0).reshape(hot_count, width)
    return (
        cold_table_new,
        cold_accum_new,
        hot_cache_new,
        hot_accum_new,
        pending_new,
        top_grad,
        out_grad,
    )


def solution(mesh):
    in_specs = (
        P(("dp", "rep"), None),
        P(("dp", "rep"), None),
        P(("dp", "rep")),
        P(("dp", "rep")),
        P(),
        P(),
        P("dp", None),
        P("dp", None),
        P(),
        P(),
        P(("dp", "rep"), None),
        P(),
        P(),
    )
    out_specs = (
        P("dp", None),
        P("dp", None),
        P(),
        P(),
        P(("dp", "rep"), None),
        P(("dp", "rep"), None),
        P(),
    )
    return jax.shard_map(local, mesh=mesh, in_specs=in_specs, out_specs=out_specs, check_vma=False)
```

profile of v0, /device:TPU:0, one launch (start us, length us, event | category | flops | bytes accessed | tf_op | source)
XLA Modules:
  0.0 244.3 jit_solution(7436814418134962637)
XLA Ops:
  8.0 1.2 copy.44
  9.4 1.1 reduce-window.6
  10.5 0.2 slice_reduce_fusion
  10.9 2.6 %scatter_custom_fusion = s32[1024]{0:T(1024)S(1)} fusion(s32[512]{0:T(512)S(1)} %bitcast.83, s32[512]{0:T(512)} %param.15, s32[]{:T(128)} %constant.13.clone.1), kind=kCustom, calls=%fused_computation.55 | custom fusion | bytes 4608 | tf_op jit(solution)/shard_map/scatter | solution.py:45
  13.5 13.6 %all_to_all.22 = s32[8,1,128]{2,1,0:T(1,128)S(1)} all-to-all(s32[8,1,128]{2,1,0:T(1,128)S(1)} %bitcast.82), channel_id=1, replica_groups=mesh['dp'=8,'rep'=4] {'dp'}, dimensions={0} | all-to-all | bytes 8192 | tf_op jit(solution)/shard_map/all_to_all | solution.py:47
  27.1 4.1 %gather_fusion.1 = bf16[1024,128]{1,0:T(8,128)(2,1)} fusion(f32[512,128]{1,0:T(8,128)S(1)} %copy-done.2, s32[1024]{0:T(1024)S(1)} %fusion.17), kind=kCustom, calls=%fused_computation.1 | custom fusion | bytes 528384 | tf_op jit(solution)/shard_map/gather | solution.py:48
  31.2 3.4 %all-to-all-start.1 = ((bf16[8,128,128]{2,1,0:T(8,128)(2,1)}), bf16[8,128,128]{2,1,0:T(8,128)(2,1)S(1)}, u32[]{:S(2)}, u32[]{:S(2)}) async-start(bf16[8,128,128]{2,1,0:T(8,128)(2,1)} %bitcast.12), calls=%async_computation.1 | async-start | bytes 524288 | tf_op jit(solution)/shard_map/all_to_all | solution.py:49
  35.0 1.1 gather_fusion
  36.0 0.5 compare_select_fusion.5
  36.6 6.2 %all-to-all-done.1 = bf16[8,128,128]{2,1,0:T(8,128)(2,1)S(1)} async-done(((bf16[8,128,128]{2,1,0:T(8,128)(2,1)}), bf16[8,128,128]{2,1,0:T(8,128)(2,1)S(1)}, u32[]{:S(2)}, u32[]{:S(2)}) %all-to-all-start.1) | async-done | bytes 262176 | tf_op jit(solution)/shard_map/all_to_all | solution.py:49
  42.8 1.3 gather_fusion.2
  44.1 0.3 pad_maximum_fusion
  44.5 0.5 multiply_convert_fusion.1
  45.2 0.5 fusion.21
  45.7 0.4 copy-done.18
  46.1 0.2 copy-done.14
  46.3 1.3 convolution_convert_fusion
  47.6 1.8 reshape.179
  49.4 1.9 fusion.20
  51.3 2.8 %scatter_custom_fusion.1 = bf16[1024,128]{1,0:T(8,128)(2,1)} fusion(s32[512]{0:T(512)S(1)} %bitcast.85, bf16[512,128]{1,0:T(8,128)(2,1)} %bitcast.77, bf16[]{:T(256)} %constant.17.clone.1), kind=kCustom, calls=%fused_computation.31 | custom fusion | bytes 262656 | tf_op jit(solution)/shard_map/scatter | solution.py:78
  54.1 4.0 %all-to-all-start.2 = ((bf16[8,128,128]{2,1,0:T(8,128)(2,1)}), bf16[8,128,128]{2,1,0:T(8,128)(2,1)}, u32[]{:S(2)}, u32[]{:S(2)}) async-start(bf16[8,128,128]{2,1,0:T(8,128)(2,1)} %bitcast.71), calls=%async_computation.2 | async-start | bytes 524288 | tf_op jit(solution)/shard_map/all_to_all | solution.py:80
  58.2 0.8 copy.22
  59.0 1.1 reshape.183
  60.0 0.6 compare_select_fusion.1
  60.6 3.6 %scatter_custom_fusion.3 = f32[1024,128]{1,0:T(8,128)S(1)} fusion(f32[1024,128]{1,0:T(8,128)S(1)} %copy-done.6, s32[512]{0:T(512)} %bitcast.91, bf16[512,128]{1,0:T(8,128)(2,1)S(1)} %bitcast.72), kind=kCustom, calls=%fused_computation.25 | custom fusion | flops 131072 | bytes 655360 | tf_op jit(solution)/shard_map/scatter-add | solution.py:100
  64.3 1.2 gather_fusion.4
  65.6 0.7 all-to-all-done.2
  66.3 7.1 %scatter_custom_fusion.2 = f32[512,128]{1,0:T(8,128)} fusion(s32[1024]{0:T(1024)S(1)} %bitcast.90, bf16[1024,128]{1,0:T(8,128)(2,1)} %bitcast.31, f32[]{:T(128)} %constant.15.clone.1), kind=kCustom, calls=%fused_computation.18 | custom fusion | flops 262144 | bytes 524292 | tf_op jit(solution)/shard_map/scatter-add | solution.py:85
  73.4 0.2 reduce-scatter.5.cloned.1.call-start
  73.7 3.4 %fusion.2 = f32[512,1024]{1,0:T(8,128)} fusion(bf16[32,8,4,128]{3,2,1,0:T(4,128)(2,1)} %bitcast.76, f32[256,1024]{1,0:T(8,128)} %copy-done.18, f32[1024]{0:T(1024)} %param.18, f32[256]{0:T(256)S(1)} %copy-done.15), kind=kOutput, calls=%fused_computation.20 | convolution fusion | flops 271056896 | bytes 3412992 | tf_op jit(solution)/shard_map/dot_general | solution.py:66
  77.1 0.6 copy-done.1
  77.7 0.6 gather_fusion.5
  78.3 1.2 gather_fusion.3
  79.6 1.2 gather_fusion.6
  80.8 0.7 broadcast.101
  81.5 1.5 scatter_fusion.2
  83.1 0.3 fusion.22
  83.4 41.0 %psum.15 = f32[1024]{0:T(1024)} all-reduce(f32[1024]{0:T(1024)S(1)} %bitcast.81), channel_id=1, replica_groups=mesh['dp'=8,'rep'=4] {'dp','rep'}, use_global_device_ids=true, to_apply=%region_13.14 | all-reduce | flops 1024 | bytes 8192 | tf_op jit(solution)/shard_map/psum | solution.py:108
  124.4 67.7 %all-reduce.2.cloned.1.call-done = f32[3,128,128]{2,1,0:T(8,128)} async-done(((f32[3,128,128]{2,1,0:T(8,128)}), f32[3,128,128]{2,1,0:T(8,128)}) %all-reduce.2.cloned.1.call-update) | async-done | bytes 196624 | tf_op jit(solution)/shard_map/psum | solution.py:108
  192.1 1.3 multiply_add_fusion
  193.4 0.7 scatter_fusion.1
  194.0 0.7 scatter_fusion
  194.8 1.1 multiply_add_fusion.1
  195.8 6.4 %all_gather.7 = f32[512,128]{1,0:T(8,128)S(1)} all-gather(f32[128,128]{1,0:T(8,128)S(1)} %get-tuple-element.9), channel_id=1, replica_groups=mesh['dp'=8,'rep'=4] {'rep'}, dimensions={0}, use_global_device_ids=true | all-gather | bytes 327680 | tf_op jit(solution)/shard_map/all_gather | solution.py:95
  202.2 6.1 %all_gather.6 = f32[512,128]{1,0:T(8,128)S(1)} all-gather(f32[128,128]{1,0:T(8,128)S(1)} %get-tuple-element.10), channel_id=1, replica_groups=mesh['dp'=8,'rep'=4] {'rep'}, dimensions={0}, use_global_device_ids=true | all-gather | bytes 327680 | tf_op jit(solution)/shard_map/all_gather | solution.py:94
  208.3 27.2 %reduce-scatter.5.cloned.1.call-done = f32[16,1024]{1,0:T(8,128)} async-done(((f32[512,1024]{1,0:T(8,128)}), f32[16,1024]{1,0:T(8,128)}) %reduce-scatter.5.cloned.1.call-update) | async-done | bytes 65552 | tf_op jit(solution)/shard_map/reduce_scatter | solution.py:65
  235.5 0.7 copy.47
  236.2 0.7 copy.48
  (57 shorter events, 1.1 us)
Async XLA Ops:
  8.0 36.4 %copy-start = (bf16[512,1024]{1,0:T(8,128)(2,1)S(1)}, bf16[512,1024]{1,0:T(8,128)(2,1)}, u32[]{:S(2)}) copy-start(bf16[512,1024]{1,0:T(8,128)(2,1)} %param.17) | copy-start | bytes 3145732
  8.0 1.4 copy-start.9
  8.0 19.1 %copy-start.2 = (f32[512,128]{1,0:T(8,128)S(1)}, f32[512,128]{1,0:T(8,128)}, u32[]{:S(2)}) copy-start(f32[512,128]{1,0:T(8,128)} %param.19) | copy-start | bytes 786436
  8.0 1.3 copy-start.7
  9.3 25.3 %copy-start.10 = (s32[256,2]{0,1:T(2,128)S(1)}, s32[256,2]{0,1:T(2,128)}, u32[]{:S(2)}) copy-start(s32[256,2]{0,1:T(2,128)} %param.13) | copy-start | bytes 6148
  27.1 8.9 %copy-start.17 = (s32[3]{0:T(128)S(1)}, s32[3]{0:T(128)}, u32[]{:S(2)}) copy-start(s32[3]{0:T(128)} %param.24) | copy-start | bytes 40
  31.2 11.6 %all-to-all-start.1 = ((bf16[8,128,128]{2,1,0:T(8,128)(2,1)}), bf16[8,128,128]{2,1,0:T(8,128)(2,1)S(1)}, u32[]{:S(2)}, u32[]{:S(2)}) async-start(bf16[8,128,128]{2,1,0:T(8,128)(2,1)} %bitcast.12), calls=%async_computation.1 | async-start | bytes 524288 | tf_op jit(solution)/shard_map/all_to_all | solution.py:49
  44.4 0.7 copy-start.8
  44.4 0.7 copy-start.13
  44.4 1.2 copy-start.16
  45.1 1.0 copy-start.18
  45.7 0.6 copy-start.14
  46.3 11.9 %copy-start.11 = (s32[3]{0:T(128)S(1)}, s32[3]{0:T(128)}, u32[]{:S(2)}) copy-start(s32[3]{0:T(128)} %compare_select_fusion.5) | copy-start | bytes 40
  47.6 13.0 %copy-start.6 = (f32[1024,128]{1,0:T(8,128)S(1)}, f32[1024,128]{1,0:T(8,128)}, u32[]{:S(2)}) copy-start(f32[1024,128]{1,0:T(8,128)} %param.23) | copy-start | bytes 1572868
  54.1 12.3 %all-to-all-start.2 = ((bf16[8,128,128]{2,1,0:T(8,128)(2,1)}), bf16[8,128,128]{2,1,0:T(8,128)(2,1)}, u32[]{:S(2)}, u32[]{:S(2)}) async-start(bf16[8,128,128]{2,1,0:T(8,128)(2,1)} %bitcast.71), calls=%async_computation.2 | async-start | bytes 524288 | tf_op jit(solution)/shard_map/all_to_all | solution.py:80
  58.1 134.0 %all-reduce.2.cloned.1.call-start = ((), (), s32[]{:S(2)}) async-start(), calls=%async_computation.6 | async-start | bytes 393216 | tf_op jit(solution)/shard_map/psum | solution.py:108
  59.0 14.7 %copy-start.15 = (f32[256]{0:T(256)S(1)}, f32[256]{0:T(256)}, u32[]{:S(2)}) copy-start(f32[256]{0:T(256)} %copy-done.14) | copy-start | bytes 3076
  65.5 129.2 %reduce-scatter.3.cloned.1.call-start = ((), (), s32[]{:S(2)}) async-start(), calls=%async_computation.5 | async-start | bytes 327680 | tf_op jit(solution)/shard_map/reduce_scatter | solution.py:89
  73.4 162.1 %reduce-scatter.5.cloned.1.call-start = ((), (), s32[]{:S(2)}) async-start(), calls=%async_computation.7 | async-start | bytes 2162688 | tf_op jit(solution)/shard_map/reduce_scatter | solution.py:65
  77.0 0.7 copy-start.1
  77.1 4.5 %copy-start.12 = (s32[3]{0:T(128)S(1)}, s32[3]{0:T(128)}, u32[]{:S(2)}) copy-start(s32[3]{0:T(128)} %compare_select_fusion.5) | copy-start | bytes 40
  83.1 153.1 %copy-start.5 = (f32[8,128,128]{2,1,0:T(8,128)}, f32[8,128,128]{2,1,0:T(8,128)S(1)}, u32[]{:S(2)}) copy-start(f32[8,128,128]{2,1,0:T(8,128)S(1)} %scatter_fusion.2) | copy-start | bytes 1572868
  194.0 42.9 %copy-start.4 = (f32[8,128,128]{2,1,0:T(8,128)}, f32[8,128,128]{2,1,0:T(8,128)S(1)}, u32[]{:S(2)}) copy-start(f32[8,128,128]{2,1,0:T(8,128)S(1)} %scatter_fusion.1) | copy-start | bytes 1572868
  194.7 42.2 %copy-start.3 = (f32[8,128,128]{2,1,0:T(8,128)}, f32[8,128,128]{2,1,0:T(8,128)S(1)}, u32[]{:S(2)}) copy-start(f32[8,128,128]{2,1,0:T(8,128)S(1)} %scatter_fusion) | copy-start | bytes 1572868
Sparse Core Ops, SparseCore 0:
  65.7 126.3 all-reduce.1
Sparse Core Ops, SparseCore 1:
  73.5 21.1 reduce-scatter.2
  97.3 138.1 reduce-scatter.4
where the time goes:
time: 245 us; the launch traced here: 244 us
  waiting for transfers between devices  102 us (42%)
  blocking collectives  67 us (27%)
  local copies, waits for them, and re-layouts  30 us (12%)
  other arithmetic  15.8 us (6%)
  between operations  15.8 us (6%)
  starting transfers between devices  7.76 us (3%)
  matrix products  6.01 us (2%)
    psum x1, waiting for transfers between devices, local(): picked_sum, out_grad = lax.psum((picked, head_term), ('dp', 'rep'))  67.7 us
    psum x1, blocking collectives, local(): picked_sum, out_grad = lax.psum((picked, head_term), ('dp', 'rep'))  41 us
    reduce_scatter x1, waiting for transfers between devices, local(): lax.psum_scatter(lax.dot_general(inputs, dhidden, (((0,), (0,)), ((), ())...  27.2 us
    all_to_all x1, blocking collectives, local(): lax.all_to_all(requests, 'dp', split_axis=0, concat_axis=0, tiled=True)  13.6 us
    scatter-add x1, other arithmetic, local(): cold_grad = jnp.zeros((own_rows, width), jnp.float32).at[asked.reshape(-1...  7.07 us
    all_gather x1, blocking collectives, local(): lax.all_gather(accum_updated, 'rep', axis=0, tiled=True)  6.39 us
    all_to_all x1, waiting for transfers between devices, local(): lax.all_to_all(found, 'dp', split_axis=0, concat_axis=0, tiled=True)  6.23 us
    all_gather x1, blocking collectives, local(): lax.all_gather(table_updated, 'rep', axis=0, tiled=True)  6.1 us
  transfers between devices with their start and end apart: 5, of which 4 were waited for; matrix products, arithmetic and copies ran while one was open for 12% of the time, Pallas kernels for 0%

commit v1 on v0

--- a/solution.py
+++ b/solution.py
@@ -105,7 +105,7 @@
     accum_blocks = hot_accum.reshape(blocks_count, BLOCK, width)
     cache_chosen = cache_blocks[refresh_blocks]
     accum_chosen = accum_blocks[refresh_blocks]
-    picked_sum, out_grad = lax.psum((picked, head_term), ("dp", "rep"))
+    picked_sum, out_grad = lax.psum(lax.psum((picked, head_term), "dp"), "rep")
     flush = picked_sum / divisors[:, None, None]
     cache_part, accum_part = adagrad(cache_chosen, accum_chosen, flush)
     hot_cache_new = cache_blocks.at[refresh_blocks].set(cache_part).reshape(hot_count, width)

time: 245 us -> 341 us (1.39)
  waiting for transfers between devices: 102 us -> 223 us
  blocking collectives: 67 us -> 37.9 us
  starting transfers between devices: 7.76 us -> 15.1 us
    reduce_scatter x1, waiting for transfers between devices: 27.2 us -> 128 us  [local(): lax.psum_scatter(lax.dot_general(inputs, dhidden, (((0,), (0,)), ((), ())...]
    psum x1 -> x2, blocking collectives: 41 us -> 25.9 us  [local(): picked_sum, out_grad = lax.psum(lax.psum((picked, head_term), 'dp'), 'rep')]
    all_to_all x1 -> x0, blocking collectives: 13.6 us -> none  [local(): lax.all_to_all(requests, 'dp', split_axis=0, concat_axis=0, tiled=True)]
    reduce_scatter x1, waiting for transfers between devices: 0.03 us -> 10.8 us  [local(): lax.psum_scatter(cold_grad, 'rep', scatter_dimension=0, tiled=True)]
    all_to_all x0 -> x1, starting transfers between devices: none -> 7.28 us  [local(): lax.all_to_all(requests, 'dp', split_axis=0, concat_axis=0, tiled=True)]
    all_to_all x0 -> x1, waiting for transfers between devices: none -> 6.1 us  [local(): lax.all_to_all(requests, 'dp', split_axis=0, concat_axis=0, tiled=True)]
    psum x1 -> x2, waiting for transfers between devices: 67.7 us -> 72.1 us  [local(): picked_sum, out_grad = lax.psum(lax.psum((picked, head_term), 'dp'), 'rep')]
  transfers between devices with their start and end apart: 5 -> 7, of which waited for: 4 -> 5; matrix products, arithmetic and copies ran while one was open for 12% -> 8% of each run, Pallas kernels for 0% -> 0%
where the time goes in v1:
time: 341 us; the launch traced here: 340 us
  waiting for transfers between devices  223 us (65%)
  blocking collectives  37.9 us (11%)
  local copies, waits for them, and re-layouts  28.7 us (8%)
  other arithmetic  15.2 us (4%)
  starting transfers between devices  15.1 us (4%)
  between operations  14.1 us (4%)
  matrix products  6 us (2%)
    reduce_scatter x1, waiting for transfers between devices, local(): lax.psum_scatter(lax.dot_general(inputs, dhidden, (((0,), (0,)), ((), ())...  128 us
    psum x2, waiting for transfers between devices, local(): picked_sum, out_grad = lax.psum(lax.psum((picked, head_term), 'dp'), 'rep')  72.1 us
    psum x2, blocking collectives, local(): picked_sum, out_grad = lax.psum(lax.psum((picked, head_term), 'dp'), 'rep')  25.9 us
    reduce_scatter x1, waiting for transfers between devices, local(): lax.psum_scatter(cold_grad, 'rep', scatter_dimension=0, tiled=True)  10.8 us
    all_to_all x1, starting transfers between devices, local(): lax.all_to_all(requests, 'dp', split_axis=0, concat_axis=0, tiled=True)  7.28 us
    scatter-add x1, other arithmetic, local(): cold_grad = jnp.zeros((own_rows, width), jnp.float32).at[asked.reshape(-1...  7.08 us
  transfers between devices with their start and end apart: 7, of which 5 were waited for; matrix products, arithmetic and copies ran while one was open for 8% of the time, Pallas kernels for 0%

profile of v1, /device:TPU:0, one launch (start us, length us, event | category | flops | bytes accessed | tf_op | source)
XLA Modules:
  0.0 340.4 jit_solution(5166659583767135999)
XLA Ops:
  7.2 1.2 copy.45
  8.6 1.1 reduce-window.6
  9.7 0.2 slice_reduce_fusion
  10.1 3.2 scatter_custom_fusion
  13.3 7.3 %all-to-all-start = ((s32[8,1,128]{2,1,0:T(1,128)}), s32[8,1,128]{2,1,0:T(1,128)S(1)}, u32[]{:S(2)}, u32[]{:S(2)}) async-start(s32[8,1,128]{2,1,0:T(1,128)} %bitcast.6), calls=%async_computation | async-start | bytes 8192 | tf_op jit(solution)/shard_map/all_to_all | solution.py:47
  20.7 0.1 reshape.193
  20.9 6.1 %all-to-all-done = s32[8,1,128]{2,1,0:T(1,128)S(1)} async-done(((s32[8,1,128]{2,1,0:T(1,128)}), s32[8,1,128]{2,1,0:T(1,128)S(1)}, u32[]{:S(2)}, u32[]{:S(2)}) %all-to-all-start) | async-done | bytes 4128 | tf_op jit(solution)/shard_map/all_to_all | solution.py:47
  27.0 4.1 %gather_fusion.1 = bf16[1024,128]{1,0:T(8,128)(2,1)} fusion(f32[512,128]{1,0:T(8,128)S(1)} %copy-done.2, s32[1024]{0:T(1024)S(1)} %fusion.17), kind=kCustom, calls=%fused_computation.1 | custom fusion | bytes 528384 | tf_op jit(solution)/shard_map/gather | solution.py:48
  31.1 3.4 %all-to-all-start.1 = ((bf16[8,128,128]{2,1,0:T(8,128)(2,1)}), bf16[8,128,128]{2,1,0:T(8,128)(2,1)S(1)}, u32[]{:S(2)}, u32[]{:S(2)}) async-start(bf16[8,128,128]{2,1,0:T(8,128)(2,1)} %bitcast.12), calls=%async_computation.1 | async-start | bytes 524288 | tf_op jit(solution)/shard_map/all_to_all | solution.py:49
  34.6 0.1 reshape.183
  34.8 1.1 gather_fusion
  35.9 0.6 compare_select_fusion.1
  36.5 6.2 %all-to-all-done.1 = bf16[8,128,128]{2,1,0:T(8,128)(2,1)S(1)} async-done(((bf16[8,128,128]{2,1,0:T(8,128)(2,1)}), bf16[8,128,128]{2,1,0:T(8,128)(2,1)S(1)}, u32[]{:S(2)}, u32[]{:S(2)}) %all-to-all-start.1) | async-done | bytes 262176 | tf_op jit(solution)/shard_map/all_to_all | solution.py:49
  42.6 1.3 gather_fusion.2
  44.0 0.3 pad_maximum_fusion
  44.3 0.5 multiply_convert_fusion.1
  45.0 0.5 fusion.21
  45.6 0.4 copy-done.16
  46.0 1.3 convolution_convert_fusion
  47.3 1.7 reshape.179
  49.0 1.9 fusion.20
  50.9 2.8 scatter_custom_fusion.1
  53.7 4.0 %all-to-all-start.2 = ((bf16[8,128,128]{2,1,0:T(8,128)(2,1)}), bf16[8,128,128]{2,1,0:T(8,128)(2,1)}, u32[]{:S(2)}, u32[]{:S(2)}) async-start(bf16[8,128,128]{2,1,0:T(8,128)(2,1)} %bitcast.71), calls=%async_computation.2 | async-start | bytes 524288 | tf_op jit(solution)/shard_map/all_to_all | solution.py:80
  57.8 3.7 %scatter_custom_fusion.3 = f32[1024,128]{1,0:T(8,128)S(1)} fusion(f32[1024,128]{1,0:T(8,128)S(1)} %copy-done.6, s32[512]{0:T(512)} %bitcast.90, bf16[512,128]{1,0:T(8,128)(2,1)S(1)} %bitcast.72), kind=kCustom, calls=%fused_computation.25 | custom fusion | flops 131072 | bytes 655360 | tf_op jit(solution)/shard_map/scatter-add | solution.py:100
  61.5 1.2 gather_fusion.4
  62.8 72.1 %all-reduce.3.cloned.1.call-done = f32[3,128,128]{2,1,0:T(8,128)} async-done(((f32[3,128,128]{2,1,0:T(8,128)}), f32[3,128,128]{2,1,0:T(8,128)}) %all-reduce.3.cloned.1.call-update) | async-done | bytes 196624 | tf_op jit(solution)/shard_map/psum | solution.py:108
  135.0 7.1 %scatter_custom_fusion.2 = f32[512,128]{1,0:T(8,128)} fusion(s32[1024]{0:T(1024)S(1)} %bitcast.89, bf16[1024,128]{1,0:T(8,128)(2,1)} %bitcast.31, f32[]{:T(128)} %constant.15.clone.1), kind=kCustom, calls=%fused_computation.18 | custom fusion | flops 262144 | bytes 524292 | tf_op jit(solution)/shard_map/scatter-add | solution.py:85
  142.1 0.2 reduce-scatter.5.cloned.1.call-start
  142.3 3.4 fusion.2
  145.7 0.6 copy-done.1
  146.3 0.6 gather_fusion.5
  146.9 1.2 gather_fusion.3
  148.2 1.2 gather_fusion.6
  149.4 0.7 broadcast.101
  150.1 1.5 scatter_fusion.2
  151.7 0.3 fusion.22
  152.0 19.7 %psum.30 = f32[1024]{0:T(1024)S(1)} all-reduce(f32[1024]{0:T(1024)S(1)} %bitcast.81), channel_id=1, replica_groups=mesh['dp'=8,'rep'=4] {'dp'}, use_global_device_ids=true, to_apply=%region_14.15 | all-reduce | flops 1024 | bytes 8192 | tf_op jit(solution)/shard_map/psum | solution.py:108
  171.7 6.2 %psum.31 = f32[1024]{0:T(1024)} all-reduce(f32[1024]{0:T(1024)S(1)} %psum.30), channel_id=1, replica_groups=mesh['dp'=8,'rep'=4] {'rep'}, use_global_device_ids=true, to_apply=%region_15.16 | all-reduce | flops 1024 | bytes 8192 | tf_op jit(solution)/shard_map/psum | solution.py:108
  177.9 1.3 multiply_add_fusion
  179.2 0.7 scatter_fusion.1
  179.9 0.7 scatter_fusion
  180.6 10.8 %reduce-scatter.3.cloned.1.call-done = f32[128,128]{1,0:T(8,128)} async-done(((f32[512,128]{1,0:T(8,128)}), f32[128,128]{1,0:T(8,128)}) %reduce-scatter.3.cloned.1.call-update) | async-done | bytes 65552 | tf_op jit(solution)/shard_map/reduce_scatter | solution.py:89
  191.4 0.9 multiply_add_fusion.1
  192.3 5.8 %all_gather.7 = f32[512,128]{1,0:T(8,128)S(1)} all-gather(f32[128,128]{1,0:T(8,128)S(1)} %get-tuple-element.9), channel_id=1, replica_groups=mesh['dp'=8,'rep'=4] {'rep'}, dimensions={0}, use_global_device_ids=true | all-gather | bytes 327680 | tf_op jit(solution)/shard_map/all_gather | solution.py:95
  198.1 6.2 %all_gather.6 = f32[512,128]{1,0:T(8,128)S(1)} all-gather(f32[128,128]{1,0:T(8,128)S(1)} %get-tuple-element.10), channel_id=1, replica_groups=mesh['dp'=8,'rep'=4] {'rep'}, dimensions={0}, use_global_device_ids=true | all-gather | bytes 327680 | tf_op jit(solution)/shard_map/all_gather | solution.py:94
  204.3 128.2 %reduce-scatter.5.cloned.1.call-done = f32[16,1024]{1,0:T(8,128)} async-done(((f32[512,1024]{1,0:T(8,128)}), f32[16,1024]{1,0:T(8,128)}) %reduce-scatter.5.cloned.1.call-update) | async-done | bytes 65552 | tf_op jit(solution)/shard_map/reduce_scatter | solution.py:65
  332.5 0.7 copy.48
  333.2 0.7 copy.49
  (58 shorter events, 1.1 us)
Async XLA Ops:
  7.2 37.1 %copy-start = (bf16[512,1024]{1,0:T(8,128)(2,1)S(1)}, bf16[512,1024]{1,0:T(8,128)(2,1)}, u32[]{:S(2)}) copy-start(bf16[512,1024]{1,0:T(8,128)(2,1)} %param.17) | copy-start | bytes 3145732
  7.2 13.4 %copy-start.10 = (s32[256,2]{0,1:T(2,128)S(1)}, s32[256,2]{0,1:T(2,128)}, u32[]{:S(2)}) copy-start(s32[256,2]{0,1:T(2,128)} %param.13) | copy-start | bytes 6148
  7.2 1.4 copy-start.9
  7.2 19.8 %copy-start.2 = (f32[512,128]{1,0:T(8,128)S(1)}, f32[512,128]{1,0:T(8,128)}, u32[]{:S(2)}) copy-start(f32[512,128]{1,0:T(8,128)} %param.19) | copy-start | bytes 786436
  7.2 1.3 copy-start.7
  13.3 13.7 %all-to-all-start = ((s32[8,1,128]{2,1,0:T(1,128)}), s32[8,1,128]{2,1,0:T(1,128)S(1)}, u32[]{:S(2)}, u32[]{:S(2)}) async-start(s32[8,1,128]{2,1,0:T(1,128)} %bitcast.6), calls=%async_computation | async-start | bytes 8192 | tf_op jit(solution)/shard_map/all_to_all | solution.py:47
  27.0 8.9 %copy-start.15 = (s32[3]{0:T(128)S(1)}, s32[3]{0:T(128)}, u32[]{:S(2)}) copy-start(s32[3]{0:T(128)} %param.24) | copy-start | bytes 40
  31.1 11.6 %all-to-all-start.1 = ((bf16[8,128,128]{2,1,0:T(8,128)(2,1)}), bf16[8,128,128]{2,1,0:T(8,128)(2,1)S(1)}, u32[]{:S(2)}, u32[]{:S(2)}) async-start(bf16[8,128,128]{2,1,0:T(8,128)(2,1)} %bitcast.12), calls=%async_computation.1 | async-start | bytes 524288 | tf_op jit(solution)/shard_map/all_to_all | solution.py:49
  44.3 0.7 copy-start.8
  44.3 0.7 copy-start.11
  44.3 1.2 copy-start.14
  45.0 1.0 copy-start.16
  45.6 1.7 copy-start.12
  46.0 11.8 %copy-start.6 = (f32[1024,128]{1,0:T(8,128)S(1)}, f32[1024,128]{1,0:T(8,128)}, u32[]{:S(2)}) copy-start(f32[1024,128]{1,0:T(8,128)} %param.23) | copy-start | bytes 1572868
  53.7 81.3 %all-to-all-start.2 = ((bf16[8,128,128]{2,1,0:T(8,128)(2,1)}), bf16[8,128,128]{2,1,0:T(8,128)(2,1)}, u32[]{:S(2)}, u32[]{:S(2)}) async-start(bf16[8,128,128]{2,1,0:T(8,128)(2,1)} %bitcast.71), calls=%async_computation.2 | async-start | bytes 524288 | tf_op jit(solution)/shard_map/all_to_all | solution.py:80
  57.7 77.1 %all-reduce.3.cloned.1.call-start = ((), (), s32[]{:S(2)}) async-start(), calls=%async_computation.6 | async-start | bytes 393216 | tf_op jit(solution)/shard_map/psum | solution.py:108
  62.7 115.2 %all-reduce.5.cloned.1.call-start = ((), (), s32[]{:S(2)}) async-start(), calls=%async_computation.7 | async-start | bytes 393216 | tf_op jit(solution)/shard_map/psum | solution.py:108
  134.9 56.5 %reduce-scatter.3.cloned.1.call-start = ((), (), s32[]{:S(2)}) async-start(), calls=%async_computation.5 | async-start | bytes 327680 | tf_op jit(solution)/shard_map/reduce_scatter | solution.py:89
  142.1 190.4 %reduce-scatter.5.cloned.1.call-start = ((), (), s32[]{:S(2)}) async-start(), calls=%async_computation.8 | async-start | bytes 2162688 | tf_op jit(solution)/shard_map/reduce_scatter | solution.py:65
  145.6 0.7 copy-start.1
  145.6 6.0 %copy-start.13 = (f32[256]{0:T(256)S(1)}, f32[256]{0:T(256)}, u32[]{:S(2)}) copy-start(f32[256]{0:T(256)} %copy-done.12) | copy-start | bytes 3076
  151.7 181.5 %copy-start.5 = (f32[8,128,128]{2,1,0:T(8,128)}, f32[8,128,128]{2,1,0:T(8,128)S(1)}, u32[]{:S(2)}) copy-start(f32[8,128,128]{2,1,0:T(8,128)S(1)} %scatter_fusion.2) | copy-start | bytes 1572868
  179.9 154.0 %copy-start.4 = (f32[8,128,128]{2,1,0:T(8,128)}, f32[8,128,128]{2,1,0:T(8,128)S(1)}, u32[]{:S(2)}) copy-start(f32[8,128,128]{2,1,0:T(8,128)S(1)} %scatter_fusion.1) | copy-start | bytes 1572868
  180.6 153.3 %copy-start.3 = (f32[8,128,128]{2,1,0:T(8,128)}, f32[8,128,128]{2,1,0:T(8,128)S(1)}, u32[]{:S(2)}) copy-start(f32[8,128,128]{2,1,0:T(8,128)S(1)} %scatter_fusion) | copy-start | bytes 1572868
Sparse Core Ops, SparseCore 0:
  62.9 71.9 all-reduce.2
  137.2 31.0 all-reduce.4
  171.3 20.0 reduce-scatter.2
  194.1 138.3 reduce-scatter.4
